TPU v7x, 256 devices: a whole 4x4x8 slice. The times are simulated.
256 devices in a mesh: fsdp: 16 (over y, x), ctx: 16 (over z, core).
Axes of the slice: x: 4, y: 4, z: 8, core: 2. Of those that a mesh axis runs over, the one named last changes fastest.
Arguments:
- queries: bfloat16 [32768, 2048], P(('fsdp', 'ctx')), may hold values from -80 to 80
- keys: bfloat16 [32768, 2048], P(('fsdp', 'ctx')), may hold values from -4 to 4
- values: bfloat16 [32768, 2048], P(('fsdp', 'ctx')), may hold values from -6 to 6
- out_weight: bfloat16 [2048, 4096], P('fsdp'), may hold values from -0.125 to 0.125
- sessions: int32 [16, 2048], P('fsdp'), may hold values from 0 to 2, never falling along the last dimension, each value on 1 to 1536 neighbouring positions
Outputs:
- output: bfloat16 [32768, 4096], P(('fsdp', 'ctx'))
Inputs may be any that keep to these rules, and one draw needn't show every extreme that they name: Along each slab the session number never falls; each of the 3 sessions holds 1 to 1536 tokens and one holds exactly 1536.
All inputs are finite; a program needn't handle non-finite values.
Results may differ from a plain program's by a relative error of at most 0.007.
Values may be sent and summed in bfloat16 or wider, within the bound.
No kernel may reach another device: no remote copies, remote signals or barrier semaphores. Data moves between devices by JAX's collectives and lax.ppermute only.
A program may use at most 128 MiB of HBM per device.

v0:
```python
import math
import jax
import jax.numpy as jnp
from jax import lax
from jax.sharding import PartitionSpec as P

HDIM = 128


def per_device(queries, keys, values, out_weight, sessions):
    tokens_here = queries.shape[0]
    width = queries.shape[1]
    heads_here = width // HDIM
    scale = 1.0 / math.sqrt(HDIM)
    slab_ids = sessions[0]
    first_token = lax.axis_index("ctx") * tokens_here
    my_positions = first_token + jnp.arange(tokens_here, dtype=jnp.int32)
    my_ids = lax.dynamic_slice_in_dim(slab_ids, first_token, tokens_here)
    query_heads = jnp.transpose(queries.reshape(tokens_here, heads_here, HDIM), (1, 0, 2))
    start_state = (
        jnp.full((heads_here, tokens_here), -1e30, jnp.float32),
        jnp.zeros((heads_here, tokens_here), jnp.float32),
        jnp.zeros((heads_here, tokens_here, HDIM), jnp.float32),
    )
    key_piece = lax.all_gather(keys, "ctx", axis=0, tiled=True)
    value_piece = lax.all_gather(values, "ctx", axis=0, tiled=True)
    count = key_piece.shape[0]
    key_positions = jnp.arange(count, dtype=jnp.int32)
    allowed = (my_ids[:, None] == slab_ids[None, :]) & (
        key_positions[None, :] <= my_positions[:, None]
    )

    def update(current):
        key_heads = jnp.transpose(key_piece.reshape(count, heads_here, HDIM), (1, 0, 2))
        value_heads = jnp.transpose(value_piece.reshape(count, heads_here, HDIM), (1, 0, 2))

        def one_head(operands):
            query_head, key_head, value_head, row_max, row_total, accum = operands
            scores = jnp.dot(query_head, key_head.T, preferred_element_type=jnp.float32) * scale
            scores = jnp.where(allowed, scores, jnp.float32(-1e30))
            new_max = jnp.maximum(row_max, jnp.max(scores, axis=1))
            weights = jnp.where(allowed, jnp.exp(scores - new_max[:, None]), jnp.float32(0.0))
            factor = jnp.exp(row_max - new_max)
            new_total = row_total * factor + jnp.sum(weights, axis=1)
            added = jnp.dot(
                weights.astype(jnp.bfloat16), value_head, preferred_element_type=jnp.float32
            )
            return (new_max, new_total, accum * factor[:, None] + added)

        return lax.map(one_head, (query_heads, key_heads, value_heads) + tuple(current))

    row_max, row_total, accum = lax.cond(
        jnp.any(allowed), update, lambda current: current, start_state
    )
    finished = accum / row_total[:, :, None]
    attended = jnp.transpose(finished, (1, 0, 2)).reshape(tokens_here, width).astype(jnp.bfloat16)
    piece = lax.all_gather(out_weight, "fsdp", axis=0, tiled=True)
    projected = jnp.dot(attended, piece, preferred_element_type=jnp.float32)
    return projected.astype(jnp.bfloat16)


def solution(mesh):
    return jax.shard_map(
        per_device,
        mesh=mesh,
        in_specs=(
            P(("fsdp", "ctx"), None),
            P(("fsdp", "ctx"), None),
            P(("fsdp", "ctx"), None),
            P("fsdp", None),
            P("fsdp", None),
        ),
        out_specs=P(("fsdp", "ctx"), None),
        check_vma=False,
    )
```

profile of v0, /device:TPU:1, one launch (start us, length us, event | category | flops | bytes accessed | tf_op | source)
XLA Modules:
  0.0 274.5 jit_solution(3808026801106439446)
XLA Ops:
  6.5 2.0 copy.8
  8.7 2.0 copy.9
  12.1 1.7 fusion.16
  15.7 63.8 %all-gather.4.cloned.1.call-done = bf16[2048,2048]{0,1:T(8,128)(2,1)} async-done(((bf16[128,2048]{0,1:T(8,128)(2,1)}), bf16[2048,2048]{0,1:T(8,128)(2,1)}) %all-gather.4.cloned.1.call-update) | async-done | bytes 8388624 | tf_op jit(solution)/shard_map/all_gather | solution.py:25
  79.5 64.4 %all-gather.6.cloned.1.call-done = bf16[2048,2048]{0,1:T(8,128)(2,1)} async-done(((bf16[128,2048]{0,1:T(8,128)(2,1)}), bf16[2048,2048]{0,1:T(8,128)(2,1)}) %all-gather.6.cloned.1.call-update) | async-done | bytes 8388624 | tf_op jit(solution)/shard_map/all_gather | solution.py:26
  143.9 86.1 %conditional.1 = (f32[16,128]{1,0:T(8,128)}, f32[16,128,128]{1,2,0:T(8,128)}) conditional(s32[]{:T(128)} %convert_element_type.18, () %tuple.17, (bf16[2048,2048]{0,1:T(8,128)(2,1)}, bf16[2048,2048]{0,1:T(8,128)(2,1)}, bf16[16,128,128]{1,2,0:T(8,128)(2,1)S(1)}, pred[128,2048]{1,0:T(32,128)(4,1)S(1)}) %tuple.49), branch_computations={%region_1.0_spmd, %region_2.7_spmd} | conditional | flops 136593792 | bytes 5349073 | solution.py:52
  143.9 86.1 %while.11 = (s32[]{:T(128)}, f32[16,128]{1,0:T(8,128)}, f32[16,128,128]{1,2,0:T(8,128)}, bf16[16,128,128]{1,2,0:T(8,128)(2,1)S(1)}, bf16[16,2048,128]{1,2,0:T(8,...) while((s32[]{:T(128)}, f32[16,128]{1,0:T(8,128)}, ...), condition=%wide.region_6.6_spmd, body=%wide.region_3.5_spmd.sunk | while | flops 136593792 | bytes 5348977 | solution.py:50
  143.9 1.5 fusion.28
  149.3 1.5 fusion.28
  154.7 1.5 fusion.28
  160.1 1.5 fusion.28
  165.5 1.5 fusion.28
  170.9 1.5 fusion.28
  176.2 1.5 fusion.28
  181.6 1.5 fusion.28
  192.4 1.5 fusion.28
  197.7 1.5 fusion.28
  203.1 1.5 fusion.28
  208.5 1.5 fusion.28
  213.9 1.5 fusion.28
  219.3 1.5 fusion.28
  224.7 1.5 fusion.28
  231.4 27.4 %all-gather.8.cloned.1.call-done = bf16[2048,4096]{1,0:T(8,128)(2,1)} async-done(((bf16[128,4096]{1,0:T(8,128)(2,1)}), bf16[2048,4096]{1,0:T(8,128)(2,1)}) %all-gather.8.cloned.1.call-update) | async-done | bytes 16777232 | tf_op jit(solution)/shard_map/all_gather | solution.py:57
  258.8 9.1 %convolution_convert_fusion = bf16[128,4096]{1,0:T(8,128)(2,1)} fusion(bf16[128,2048]{0,1:T(8,128)(2,1)S(1)} %bitcast.45, bf16[2048,4096]{1,0:T(8,128)(2,1)} %all-gather.8.cloned.1.call-done), kind=kOutput, calls=%fused_computation.22 | convolution fusion | flops 2148007936 | bytes 18350080 | tf_op jit(solution)/shard_map/dot_general | solution.py:58
  (125 shorter events, 67.7 us)
Async XLA Ops:
  6.5 73.0 %all-gather.4.cloned.1.call-start = ((), (), s32[]{:S(2)}) async-start(), calls=%async_computation | async-start | bytes 8912896 | tf_op jit(solution)/shard_map/all_gather | solution.py:25
  8.6 135.3 %all-gather.6.cloned.1.call-start = ((), (), s32[]{:S(2)}) async-start(), calls=%async_computation.1 | async-start | bytes 8912896 | tf_op jit(solution)/shard_map/all_gather | solution.py:26
  10.7 248.1 %all-gather.8.cloned.1.call-start = ((), (), s32[]{:S(2)}) async-start(), calls=%async_computation.2 | async-start | bytes 17825792 | tf_op jit(solution)/shard_map/all_gather | solution.py:57
Sparse Core Ops, SparseCore 0:
  9.1 70.3 all-gather.3
  81.2 62.6 all-gather.5
  146.4 112.4 all-gather.7
where the time goes:
time: 277 us; the launch traced here: 274 us
  waiting for transfers between devices  156 us (56%)
  matrix products  56 us (20%)
  local copies, waits for them, and re-layouts  38.5 us (14%)
  between operations  13.7 us (5%)
  other arithmetic  9.54 us (3%)
    all_gather x1, waiting for transfers between devices, per_device(): value_piece = lax.all_gather(values, 'ctx', axis=0, tiled=True)  64.4 us
    all_gather x1, waiting for transfers between devices, per_device(): key_piece = lax.all_gather(keys, 'ctx', axis=0, tiled=True)  63.8 us
    dynamic_update_slice x48, local copies, waits for them, and re-layouts, update(): lax.map(one_head, (query_heads, key_heads, value_heads) + tuple(current))  32.4 us
    all_gather x1, waiting for transfers between devices, per_device(): piece = lax.all_gather(out_weight, 'fsdp', axis=0, tiled=True)  27.4 us
    dot_general x16, matrix products, one_head(): jnp.dot(query_head, key_head.T, preferred_element_type=jnp.float32) * scale  23.7 us
    dot_general x16, matrix products, one_head(): jnp.dot(weights.astype(jnp.bfloat16), value_head, preferred_element_type=...  23.2 us
    dot_general x1, matrix products, per_device(): projected = jnp.dot(attended, piece, preferred_element_type=jnp.float32)  9.1 us
    reduce_sum x16, other arithmetic, one_head(): new_total = row_total * factor + jnp.sum(weights, axis=1)  6.21 us
  transfers between devices with their start and end apart: 3, of which 3 were waited for; matrix products, arithmetic and copies ran while one was open for 34% of the time, Pallas kernels for 0%

commit v1 on v0

--- a/solution.py
+++ b/solution.py
@@ -54,7 +54,26 @@
     )
     finished = accum / row_total[:, :, None]
     attended = jnp.transpose(finished, (1, 0, 2)).reshape(tokens_here, width).astype(jnp.bfloat16)
-    piece = lax.all_gather(out_weight, "fsdp", axis=0, tiled=True)
+    count_2, position, span = (lax.axis_size("fsdp"), lax.axis_index("fsdp"), out_weight.shape[0])
+    right = [(i, (i + 1) % count_2) for i in range(count_2)]
+    left = [(i, (i - 1) % count_2) for i in range(count_2)]
+    out = jnp.zeros(
+        (*out_weight.shape[:0], count_2 * span, *out_weight.shape[0 + 1 :]), out_weight.dtype
+    )
+    out = lax.dynamic_update_slice_in_dim(out, out_weight, position * span, axis=0)
+    from_left = from_right = out_weight
+    half = count_2 // 2
+    for lap in range(1, half + 1):
+        from_left = lax.ppermute(from_left, "fsdp", right)
+        out = lax.dynamic_update_slice_in_dim(
+            out, from_left, (position - lap) % count_2 * span, axis=0
+        )
+        if lap < count_2 - half:
+            from_right = lax.ppermute(from_right, "fsdp", left)
+            out = lax.dynamic_update_slice_in_dim(
+                out, from_right, (position + lap) % count_2 * span, axis=0
+            )
+    piece = out
     projected = jnp.dot(attended, piece, preferred_element_type=jnp.float32)
     return projected.astype(jnp.bfloat16)
 

time: 277 us -> 320 us (1.16)
  the two profiles are of different devices: /device:TPU:1 before, /device:TPU:128 now
where the time goes in v1:
time: 320 us; the launch traced here: 318 us
  waiting for transfers between devices  132 us (41%)
  local copies, waits for them, and re-layouts  67.5 us (21%)
  matrix products  56.1 us (18%)
  starting transfers between devices  38.8 us (12%)
  between operations  14.1 us (4%)
  other arithmetic  8.87 us (3%)
    ppermute x8, waiting for transfers between devices, per_device(): from_left = lax.ppermute(from_left, 'fsdp', right)  123 us
    ppermute x7, starting transfers between devices, per_device(): from_right = lax.ppermute(from_right, 'fsdp', left)  37.2 us
    dynamic_update_slice x48, local copies, waits for them, and re-layouts, update(): lax.map(one_head, (query_heads, key_heads, value_heads) + tuple(current))  32.4 us
    dot_general x16, matrix products, one_head(): jnp.dot(query_head, key_head.T, preferred_element_type=jnp.float32) * scale  23.9 us
    dot_general x16, matrix products, one_head(): jnp.dot(weights.astype(jnp.bfloat16), value_head, preferred_element_type=...  23.1 us
    dynamic_update_slice x7, local copies, waits for them, and re-layouts, per_device(): lax.dynamic_update_slice_in_dim(out, from_right, (position + lap) % count...  11.2 us
    dynamic_update_slice x8, local copies, waits for them, and re-layouts, per_device(): lax.dynamic_update_slice_in_dim(out, from_left, (position - lap) % count_...  9.92 us
    ppermute x7, waiting for transfers between devices, per_device(): from_right = lax.ppermute(from_right, 'fsdp', left)  9.38 us
  transfers between devices with their start and end apart: 17, of which 12 were waited for; matrix products, arithmetic and copies ran while one was open for 11% of the time, Pallas kernels for 0%

profile of v1, /device:TPU:128, one launch (start us, length us, event | category | flops | bytes accessed | tf_op | source)
XLA Modules:
  0.0 317.9 jit_solution(12073623276625316916)
XLA Ops:
  12.4 3.9 %collective-permute-start.1 = (bf16[128,4096]{1,0:T(8,128)(2,1)}, bf16[128,4096]{1,0:T(8,128)(2,1)}, u32[]{:S(2)}, u32[]{:S(2)}) collective-permute-start(bf16[128,4096]{1,0:T(8,128)(2,1)} %param.12), channel_id=1, source_target_pairs={{0,240},{16,0},{32,16},{48,32},{64,48},{80,64},{96,80},{112,96},{1... | collective-permute-start | bytes 3145736 | tf_op jit(solution)/shard_map/ppermute | solution.py:72
  16.2 23.2 %collective-permute-done = bf16[128,4096]{1,0:T(8,128)(2,1)S(1)} collective-permute-done((bf16[128,4096]{1,0:T(8,128)(2,1)}, bf16[128,4096]{1,0:T(8,128)(2,1)S(1)}, u32[]{:S(2)}, u32[]{:S(2)}) %collective-permute-start) | collective-permute-done | bytes 1048608 | tf_op jit(solution)/shard_map/ppermute | solution.py:67
  39.5 5.3 %collective-permute-start.3 = (bf16[128,4096]{1,0:T(8,128)(2,1)}, bf16[128,4096]{1,0:T(8,128)(2,1)}, u32[]{:S(2)}, u32[]{:S(2)}) collective-permute-start(bf16[128,4096]{1,0:T(8,128)(2,1)} %collective-permute-done.1), channel_id=1, source_target_pairs={{0,240},{16,0},{32,16},{48,32},{64,48},{80,64},{96,80},{112,96},{1... | collective-permute-start | bytes 3145736 | tf_op jit(solution)/shard_map/ppermute | solution.py:72
  44.8 22.2 %collective-permute-done.2 = bf16[128,4096]{1,0:T(8,128)(2,1)S(1)} collective-permute-done((bf16[128,4096]{1,0:T(8,128)(2,1)S(1)}, bf16[128,4096]{1,0:T(8,128)(2,1)S(1)}, u32[]{:S(2)}, u32[]{:S(2)}) %collective-permute-start.2) | collective-permute-done | bytes 1048608 | tf_op jit(solution)/shard_map/ppermute | solution.py:67
  67.7 5.3 %collective-permute-start.5 = (bf16[128,4096]{1,0:T(8,128)(2,1)}, bf16[128,4096]{1,0:T(8,128)(2,1)}, u32[]{:S(2)}, u32[]{:S(2)}) collective-permute-start(bf16[128,4096]{1,0:T(8,128)(2,1)} %collective-permute-done.3), channel_id=1, source_target_pairs={{0,240},{16,0},{32,16},{48,32},{64,48},{80,64},{96,80},{112,96},{1... | collective-permute-start | bytes 3145736 | tf_op jit(solution)/shard_map/ppermute | solution.py:72
  73.0 6.0 %broadcast_in_dim.23 = bf16[2048,4096]{1,0:T(8,128)(2,1)} broadcast(bf16[]{:T(256)} %constant.136.clone.1), dimensions={} | broadcast | bytes 16777218 | tf_op jit(solution)/shard_map/broadcast_in_dim | solution.py:60
  80.1 13.5 %collective-permute-done.4 = bf16[128,4096]{1,0:T(8,128)(2,1)S(1)} collective-permute-done((bf16[128,4096]{1,0:T(8,128)(2,1)S(1)}, bf16[128,4096]{1,0:T(8,128)(2,1)S(1)}, u32[]{:S(2)}, u32[]{:S(2)}) %collective-permute-start.4) | collective-permute-done | bytes 1048608 | tf_op jit(solution)/shard_map/ppermute | solution.py:67
  99.6 5.4 %collective-permute-start.7 = (bf16[128,4096]{1,0:T(8,128)(2,1)}, bf16[128,4096]{1,0:T(8,128)(2,1)S(1)}, u32[]{:S(2)}, u32[]{:S(2)}) collective-permute-start(bf16[128,4096]{1,0:T(8,128)(2,1)} %collective-permute-done.5), channel_id=1, source_target_pairs={{0,240},{16,0},{32,16},{48,32},{64,48},{80,64},{96,80},{112,96},{1... | collective-permute-start | bytes 3145736 | tf_op jit(solution)/shard_map/ppermute | solution.py:72
  105.0 2.3 constant_dynamic-update-slice_fusion.14
  107.3 12.0 %collective-permute-done.6 = bf16[128,4096]{1,0:T(8,128)(2,1)S(1)} collective-permute-done((bf16[128,4096]{1,0:T(8,128)(2,1)S(1)}, bf16[128,4096]{1,0:T(8,128)(2,1)S(1)}, u32[]{:S(2)}, u32[]{:S(2)}) %collective-permute-start.6) | collective-permute-done | bytes 1048608 | tf_op jit(solution)/shard_map/ppermute | solution.py:67
  120.4 2.3 constant_dynamic-update-slice_fusion.12
  122.6 2.3 collective-permute-done.7
  124.9 5.7 %collective-permute-start.9 = (bf16[128,4096]{1,0:T(8,128)(2,1)S(1)}, bf16[128,4096]{1,0:T(8,128)(2,1)S(1)}, u32[]{:S(2)}, u32[]{:S(2)}) collective-permute-start(bf16[128,4096]{1,0:T(8,128)(2,1)S(1)} %collective-permute-done.7), channel_id=1, source_target_pairs={{0,240},{16,0},{32,16},{48,32},{64,48},{80,64},{96,80},{112,96},{1... | collective-permute-start | bytes 3145736 | tf_op jit(solution)/shard_map/ppermute | solution.py:72
  131.7 12.3 %collective-permute-done.8 = bf16[128,4096]{1,0:T(8,128)(2,1)S(1)} collective-permute-done((bf16[128,4096]{1,0:T(8,128)(2,1)S(1)}, bf16[128,4096]{1,0:T(8,128)(2,1)S(1)}, u32[]{:S(2)}, u32[]{:S(2)}) %collective-permute-start.8) | collective-permute-done | bytes 1048608 | tf_op jit(solution)/shard_map/ppermute | solution.py:67
  144.0 2.3 constant_dynamic-update-slice_fusion.10
  149.3 5.8 %collective-permute-start.11 = (bf16[128,4096]{1,0:T(8,128)(2,1)S(1)}, bf16[128,4096]{1,0:T(8,128)(2,1)S(1)}, u32[]{:S(2)}, u32[]{:S(2)}) collective-permute-start(bf16[128,4096]{1,0:T(8,128)(2,1)S(1)} %collective-permute-done.9), channel_id=1, source_target_pairs={{0,240},{16,0},{32,16},{48,32},{64,48},{80,64},{96,80},{112,96},{1... | collective-permute-start | bytes 3145736 | tf_op jit(solution)/shard_map/ppermute | solution.py:72
  156.2 11.7 %collective-permute-done.10 = bf16[128,4096]{1,0:T(8,128)(2,1)S(1)} collective-permute-done((bf16[128,4096]{1,0:T(8,128)(2,1)S(1)}, bf16[128,4096]{1,0:T(8,128)(2,1)S(1)}, u32[]{:S(2)}, u32[]{:S(2)}) %collective-permute-start.10) | collective-permute-done | bytes 1048608 | tf_op jit(solution)/shard_map/ppermute | solution.py:67
  170.0 2.9 collective-permute-done.11
  172.9 5.8 %collective-permute-start.13 = (bf16[128,4096]{1,0:T(8,128)(2,1)S(1)}, bf16[128,4096]{1,0:T(8,128)(2,1)S(1)}, u32[]{:S(2)}, u32[]{:S(2)}) collective-permute-start(bf16[128,4096]{1,0:T(8,128)(2,1)S(1)} %collective-permute-done.11), channel_id=1, source_target_pairs={{0,240},{16,0},{32,16},{48,32},{64,48},{80,64},{96,80},{112,96},{1... | collective-permute-start | bytes 3145736 | tf_op jit(solution)/shard_map/ppermute | solution.py:72
  179.8 11.4 %collective-permute-done.12 = bf16[128,4096]{1,0:T(8,128)(2,1)S(1)} collective-permute-done((bf16[128,4096]{1,0:T(8,128)(2,1)S(1)}, bf16[128,4096]{1,0:T(8,128)(2,1)S(1)}, u32[]{:S(2)}, u32[]{:S(2)}) %collective-permute-start.12) | collective-permute-done | bytes 1048608 | tf_op jit(solution)/shard_map/ppermute | solution.py:67
  196.7 16.5 %collective-permute-done.14 = bf16[128,4096]{1,0:T(8,128)(2,1)S(1)} collective-permute-done((bf16[128,4096]{1,0:T(8,128)(2,1)S(1)}, bf16[128,4096]{1,0:T(8,128)(2,1)S(1)}, u32[]{:S(2)}, u32[]{:S(2)}) %collective-permute-start.14) | collective-permute-done | bytes 1048608 | tf_op jit(solution)/shard_map/ppermute | solution.py:67
  214.4 86.2 %conditional.1 = (f32[16,128]{1,0:T(8,128)}, f32[16,128,128]{1,2,0:T(8,128)}) conditional(s32[]{:T(128)} %convert_element_type.18, () %tuple.17, (bf16[2048,2048]{0,1:T(8,128)(2,1)}, bf16[2048,2048]{0,1:T(8,128)(2,1)}, bf16[16,128,128]{1,2,0:T(8,128)(2,1)}, pred[128,2048]{1,0:T(32,128)(4,1)S(1)}) %tuple.47), branch_computations={%region_1.0_spmd, %region_2.7_spmd} | conditional | flops 136593792 | bytes 5349073 | solution.py:52
  214.4 86.2 %while.11 = (s32[]{:T(128)}, f32[16,128]{1,0:T(8,128)}, f32[16,128,128]{1,2,0:T(8,128)}, bf16[16,128,128]{1,2,0:T(8,128)(2,1)}, bf16[16,2048,128]{1,2,0:T(8,128)...) while((s32[]{:T(128)}, f32[16,128]{1,0:T(8,128)}, ...), condition=%wide.region_6.6_spmd, body=%wide.region_3.5_spmd.sunk | while | flops 136593792 | bytes 5348977 | solution.py:50
  302.0 9.1 %convolution_convert_fusion = bf16[128,4096]{1,0:T(8,128)(2,1)} fusion(bf16[128,2048]{0,1:T(8,128)(2,1)S(1)} %bitcast.45, bf16[2048,4096]{1,0:T(8,128)(2,1)} %constant_dynamic-update-slice_fusion.1), kind=kOutput, calls=%fused_computation.22 | convolution fusion | flops 2148007936 | bytes 18350080 | tf_op jit(solution)/shard_map/dot_general | solution.py:77
  (175 shorter events, 116.4 us)
Async XLA Ops:
  6.5 72.4 %copy-start = (bf16[128,4096]{1,0:T(8,128)(2,1)S(1)}, bf16[128,4096]{1,0:T(8,128)(2,1)}, u32[]{:S(2)}) copy-start(bf16[128,4096]{1,0:T(8,128)(2,1)} %param.12) | copy-start | bytes 3145732
  6.5 87.1 %copy-start.2 = (s32[1,2048]{1,0:T(1,128)S(1)}, s32[1,2048]{1,0:T(1,128)}, u32[]{:S(2)}) copy-start(s32[1,2048]{1,0:T(1,128)} %param.13) | copy-start | bytes 24580
  6.5 207.9 %all-gather.3.cloned.1.call-start = ((), (), s32[]{:S(2)}) async-start(), calls=%async_computation | async-start | bytes 8912896 | tf_op jit(solution)/shard_map/all_gather | solution.py:25
  8.7 205.7 %all-gather.5.cloned.1.call-start = ((), (), s32[]{:S(2)}) async-start(), calls=%async_computation.1 | async-start | bytes 8912896 | tf_op jit(solution)/shard_map/all_gather | solution.py:26
  10.8 28.7 %collective-permute-start = (bf16[128,4096]{1,0:T(8,128)(2,1)}, bf16[128,4096]{1,0:T(8,128)(2,1)S(1)}, u32[]{:S(2)}, u32[]{:S(2)}) collective-permute-start(bf16[128,4096]{1,0:T(8,128)(2,1)} %param.12), channel_id=1, source_target_pairs={{0,16},{16,32},{32,48},{48,64},{64,80},{80,96},{96,112},{112,128},... | collective-permute-start | bytes 3145736 | tf_op jit(solution)/shard_map/ppermute | solution.py:67
  12.4 27.1 %collective-permute-start.1 = (bf16[128,4096]{1,0:T(8,128)(2,1)}, bf16[128,4096]{1,0:T(8,128)(2,1)}, u32[]{:S(2)}, u32[]{:S(2)}) collective-permute-start(bf16[128,4096]{1,0:T(8,128)(2,1)} %param.12), channel_id=1, source_target_pairs={{0,240},{16,0},{32,16},{48,32},{64,48},{80,64},{96,80},{112,96},{1... | collective-permute-start | bytes 3145736 | tf_op jit(solution)/shard_map/ppermute | solution.py:72
  39.5 5.4 %copy-start.1 = (bf16[128,4096]{1,0:T(8,128)(2,1)}, bf16[128,4096]{1,0:T(8,128)(2,1)S(1)}, u32[]{:S(2)}) copy-start(bf16[128,4096]{1,0:T(8,128)(2,1)S(1)} %collective-permute-done) | copy-start | bytes 3145732
  39.5 27.5 %collective-permute-start.2 = (bf16[128,4096]{1,0:T(8,128)(2,1)S(1)}, bf16[128,4096]{1,0:T(8,128)(2,1)S(1)}, u32[]{:S(2)}, u32[]{:S(2)}) collective-permute-start(bf16[128,4096]{1,0:T(8,128)(2,1)S(1)} %collective-permute-done), channel_id=1, source_target_pairs={{0,16},{16,32},{32,48},{48,64},{64,80},{80,96},{96,112},{112,128},... | collective-permute-start | bytes 3145736 | tf_op jit(solution)/shard_map/ppermute | solution.py:67
  39.5 28.2 %collective-permute-start.3 = (bf16[128,4096]{1,0:T(8,128)(2,1)}, bf16[128,4096]{1,0:T(8,128)(2,1)}, u32[]{:S(2)}, u32[]{:S(2)}) collective-permute-start(bf16[128,4096]{1,0:T(8,128)(2,1)} %collective-permute-done.1), channel_id=1, source_target_pairs={{0,240},{16,0},{32,16},{48,32},{64,48},{80,64},{96,80},{112,96},{1... | collective-permute-start | bytes 3145736 | tf_op jit(solution)/shard_map/ppermute | solution.py:72
  67.0 26.6 %collective-permute-start.4 = (bf16[128,4096]{1,0:T(8,128)(2,1)S(1)}, bf16[128,4096]{1,0:T(8,128)(2,1)S(1)}, u32[]{:S(2)}, u32[]{:S(2)}) collective-permute-start(bf16[128,4096]{1,0:T(8,128)(2,1)S(1)} %collective-permute-done.2), channel_id=1, source_target_pairs={{0,16},{16,32},{32,48},{48,64},{64,80},{80,96},{96,112},{112,128},... | collective-permute-start | bytes 3145736 | tf_op jit(solution)/shard_map/ppermute | solution.py:67
  67.7 32.0 %collective-permute-start.5 = (bf16[128,4096]{1,0:T(8,128)(2,1)}, bf16[128,4096]{1,0:T(8,128)(2,1)}, u32[]{:S(2)}, u32[]{:S(2)}) collective-permute-start(bf16[128,4096]{1,0:T(8,128)(2,1)} %collective-permute-done.3), channel_id=1, source_target_pairs={{0,240},{16,0},{32,16},{48,32},{64,48},{80,64},{96,80},{112,96},{1... | collective-permute-start | bytes 3145736 | tf_op jit(solution)/shard_map/ppermute | solution.py:72
  93.6 25.7 %collective-permute-start.6 = (bf16[128,4096]{1,0:T(8,128)(2,1)S(1)}, bf16[128,4096]{1,0:T(8,128)(2,1)S(1)}, u32[]{:S(2)}, u32[]{:S(2)}) collective-permute-start(bf16[128,4096]{1,0:T(8,128)(2,1)S(1)} %collective-permute-done.4), channel_id=1, source_target_pairs={{0,16},{16,32},{32,48},{48,64},{64,80},{80,96},{96,112},{112,128},... | collective-permute-start | bytes 3145736 | tf_op jit(solution)/shard_map/ppermute | solution.py:67
  99.6 25.3 %collective-permute-start.7 = (bf16[128,4096]{1,0:T(8,128)(2,1)}, bf16[128,4096]{1,0:T(8,128)(2,1)S(1)}, u32[]{:S(2)}, u32[]{:S(2)}) collective-permute-start(bf16[128,4096]{1,0:T(8,128)(2,1)} %collective-permute-done.5), channel_id=1, source_target_pairs={{0,240},{16,0},{32,16},{48,32},{64,48},{80,64},{96,80},{112,96},{1... | collective-permute-start | bytes 3145736 | tf_op jit(solution)/shard_map/ppermute | solution.py:72
  119.3 24.8 %collective-permute-start.8 = (bf16[128,4096]{1,0:T(8,128)(2,1)S(1)}, bf16[128,4096]{1,0:T(8,128)(2,1)S(1)}, u32[]{:S(2)}, u32[]{:S(2)}) collective-permute-start(bf16[128,4096]{1,0:T(8,128)(2,1)S(1)} %collective-permute-done.6), channel_id=1, source_target_pairs={{0,16},{16,32},{32,48},{48,64},{64,80},{80,96},{96,112},{112,128},... | collective-permute-start | bytes 3145736 | tf_op jit(solution)/shard_map/ppermute | solution.py:67
  124.9 24.4 %collective-permute-start.9 = (bf16[128,4096]{1,0:T(8,128)(2,1)S(1)}, bf16[128,4096]{1,0:T(8,128)(2,1)S(1)}, u32[]{:S(2)}, u32[]{:S(2)}) collective-permute-start(bf16[128,4096]{1,0:T(8,128)(2,1)S(1)} %collective-permute-done.7), channel_id=1, source_target_pairs={{0,240},{16,0},{32,16},{48,32},{64,48},{80,64},{96,80},{112,96},{1... | collective-permute-start | bytes 3145736 | tf_op jit(solution)/shard_map/ppermute | solution.py:72
  144.0 23.8 %collective-permute-start.10 = (bf16[128,4096]{1,0:T(8,128)(2,1)S(1)}, bf16[128,4096]{1,0:T(8,128)(2,1)S(1)}, u32[]{:S(2)}, u32[]{:S(2)}) collective-permute-start(bf16[128,4096]{1,0:T(8,128)(2,1)S(1)} %collective-permute-done.8), channel_id=1, source_target_pairs={{0,16},{16,32},{32,48},{48,64},{64,80},{80,96},{96,112},{112,128},... | collective-permute-start | bytes 3145736 | tf_op jit(solution)/shard_map/ppermute | solution.py:67
  149.3 23.6 %collective-permute-start.11 = (bf16[128,4096]{1,0:T(8,128)(2,1)S(1)}, bf16[128,4096]{1,0:T(8,128)(2,1)S(1)}, u32[]{:S(2)}, u32[]{:S(2)}) collective-permute-start(bf16[128,4096]{1,0:T(8,128)(2,1)S(1)} %collective-permute-done.9), channel_id=1, source_target_pairs={{0,240},{16,0},{32,16},{48,32},{64,48},{80,64},{96,80},{112,96},{1... | collective-permute-start | bytes 3145736 | tf_op jit(solution)/shard_map/ppermute | solution.py:72
  167.8 23.3 %collective-permute-start.12 = (bf16[128,4096]{1,0:T(8,128)(2,1)S(1)}, bf16[128,4096]{1,0:T(8,128)(2,1)S(1)}, u32[]{:S(2)}, u32[]{:S(2)}) collective-permute-start(bf16[128,4096]{1,0:T(8,128)(2,1)S(1)} %collective-permute-done.10), channel_id=1, source_target_pairs={{0,16},{16,32},{32,48},{48,64},{64,80},{80,96},{96,112},{112,128},... | collective-permute-start | bytes 3145736 | tf_op jit(solution)/shard_map/ppermute | solution.py:67
  172.9 22.7 %collective-permute-start.13 = (bf16[128,4096]{1,0:T(8,128)(2,1)S(1)}, bf16[128,4096]{1,0:T(8,128)(2,1)S(1)}, u32[]{:S(2)}, u32[]{:S(2)}) collective-permute-start(bf16[128,4096]{1,0:T(8,128)(2,1)S(1)} %collective-permute-done.11), channel_id=1, source_target_pairs={{0,240},{16,0},{32,16},{48,32},{64,48},{80,64},{96,80},{112,96},{1... | collective-permute-start | bytes 3145736 | tf_op jit(solution)/shard_map/ppermute | solution.py:72
  191.2 22.1 %collective-permute-start.14 = (bf16[128,4096]{1,0:T(8,128)(2,1)S(1)}, bf16[128,4096]{1,0:T(8,128)(2,1)S(1)}, u32[]{:S(2)}, u32[]{:S(2)}) collective-permute-start(bf16[128,4096]{1,0:T(8,128)(2,1)S(1)} %collective-permute-done.12), channel_id=1, source_target_pairs={{0,16},{16,32},{32,48},{48,64},{64,80},{80,96},{96,112},{112,128},... | collective-permute-start | bytes 3145736 | tf_op jit(solution)/shard_map/ppermute | solution.py:67
Sparse Core Ops, SparseCore 0:
  9.1 62.5 all-gather.2
  73.5 62.6 all-gather.4
